TPU v7x, 32 devices: a whole 2x2x4 slice. The times are simulated.
32 devices in a mesh: ctx: 8 (over z, x), tp: 4 (over y, core).
Axes of the slice: x: 2, y: 2, z: 4, core: 2. Of those that a mesh axis runs over, the one named last changes fastest.
Arguments:
- queries: bfloat16 [1024, 1024], P('ctx', 'tp'), may hold values from -6 to 6
- keys: bfloat16 [1024, 1024], P('ctx', 'tp'), may hold values from -6 to 6
- values: bfloat16 [1024, 1024], P('ctx', 'tp'), may hold values from -6 to 6
- utterance: int32 [1024], P('ctx'), may hold values from 0 to 5, never falling along the last dimension, each value on 1 to 768 neighbouring positions
- w_out: bfloat16 [1024, 1536], P('tp'), may hold values from -0.5 to 0.5
- cotangent: bfloat16 [1024, 1536], P('ctx', 'tp'), may hold values from -2.5 to 2.5
Outputs:
- output: bfloat16 [1024, 1536], P('ctx', 'tp')
- grad_queries: bfloat16 [1024, 1024], P('ctx', 'tp')
- grad_keys: bfloat16 [1024, 1024], P('ctx', 'tp')
- grad_values: bfloat16 [1024, 1024], P('ctx', 'tp')
Inputs may be any that keep to these rules, and one draw needn't show every extreme that they name: `utterance`: utterance numbers never fall along the frames; each of the 6 utterances covers 1 to 768 frames, and one covers exactly 768.
All inputs are finite; a program needn't handle non-finite values.
Results may differ from a plain program's by a relative error of at most 0.034.
Values may be sent and summed in bfloat16 or wider, within the bound.
A program may use at most 64 MiB of HBM per device.

v0:
```python
import jax
import jax.numpy as jnp
from jax import lax
from jax.sharding import PartitionSpec as P

HS = 64


NEGATIVE = -1e30


def split_pair(values32):
    upper_part = values32.astype(jnp.bfloat16)
    widened = lax.optimization_barrier(upper_part).astype(jnp.float32)
    return (upper_part, (values32 - widened).astype(jnp.bfloat16))


def joined(upper_part, lower_part):
    return upper_part.astype(jnp.float32) + lower_part.astype(jnp.float32)


def by_blocks(advance, running, pieces):
    row_count = pieces[0].shape[0]
    stacked = tuple(
        (member.reshape((row_count // 512, 512) + member.shape[1:]) for member in pieces)
    )

    def one_turn(current, block_in):
        return (advance(current, block_in), None)

    running, unused = lax.scan(one_turn, running, stacked)
    return running


def shards(queries, keys, values, utterance, w_out, cotangent):
    inv_root = HS ** (-0.5)
    frame_count = queries.shape[0]
    local_heads = queries.shape[1] // HS
    query_heads = queries.reshape(frame_count, local_heads, HS)
    key_heads = keys.reshape(frame_count, local_heads, HS)
    value_heads = values.reshape(frame_count, local_heads, HS)

    def forward_step(running, pieces):
        key_piece, value_piece, piece_ids = pieces
        piece_rows = key_piece.shape[0]
        key_part = key_piece.reshape(piece_rows, local_heads, HS)
        value_part = value_piece.reshape(piece_rows, local_heads, HS)
        row_top, totals, mixture = running
        scores = (
            jnp.einsum("qhd,khd->hqk", query_heads, key_part, preferred_element_type=jnp.float32)
            * inv_root
        )
        same_utt = (utterance[:, None] == piece_ids[None, :])[None]
        masked = jnp.where(same_utt, scores, NEGATIVE)
        new_top = jnp.maximum(row_top, jnp.max(masked, axis=2))
        weights = jnp.where(same_utt, jnp.exp(masked - new_top[:, :, None]), 0.0)
        factor = jnp.exp(row_top - new_top)
        totals = totals * factor + jnp.sum(weights, axis=2)
        mixture = mixture * factor[:, :, None] + jnp.einsum(
            "hqk,khd->hqd",
            weights.astype(jnp.bfloat16),
            value_part,
            preferred_element_type=jnp.float32,
        )
        return (new_top, totals, mixture)

    start_top = jnp.full((local_heads, frame_count), NEGATIVE, jnp.float32)
    start_sum = jnp.zeros((local_heads, frame_count), jnp.float32)
    empty_heads = jnp.zeros((local_heads, frame_count, HS), jnp.float32)
    row_top, totals, mixture = by_blocks(
        forward_step,
        (start_top, start_sum, empty_heads),
        (
            lax.all_gather(keys, "ctx", axis=0, tiled=True),
            lax.all_gather(values, "ctx", axis=0, tiled=True),
            lax.all_gather(utterance, "ctx", axis=0, tiled=True),
        ),
    )
    attn_heads = mixture / totals[:, :, None]
    attn = attn_heads.transpose(1, 0, 2).reshape(frame_count, local_heads * HS).astype(jnp.bfloat16)
    projected = jnp.dot(attn, w_out, preferred_element_type=jnp.float32)
    output = lax.psum_scatter(projected.astype(jnp.bfloat16), "tp", scatter_dimension=1, tiled=True)
    lse_upper, lse_lower = split_pair((row_top + jnp.log(totals)).T)
    attn_grad = lax.dot_general(
        lax.all_gather(cotangent, "tp", axis=1, tiled=True),
        w_out,
        (((1,), (1,)), ((), ())),
        preferred_element_type=jnp.float32,
    ).astype(jnp.bfloat16)
    grad_heads = attn_grad.reshape(frame_count, local_heads, HS)
    delta = jnp.sum(
        grad_heads.astype(jnp.float32)
        * attn.reshape(frame_count, local_heads, HS).astype(jnp.float32),
        axis=2,
    )
    delta_upper, delta_lower = split_pair(delta)
    lse_local = joined(lse_upper, lse_lower).T
    delta_local = joined(delta_upper, delta_lower).T

    def query_side(running, pieces):
        key_piece, value_piece, piece_ids = pieces
        piece_rows = key_piece.shape[0]
        key_part = key_piece.reshape(piece_rows, local_heads, HS)
        value_part = value_piece.reshape(piece_rows, local_heads, HS)
        scores = (
            jnp.einsum("qhd,khd->hqk", query_heads, key_part, preferred_element_type=jnp.float32)
            * inv_root
        )
        same_utt = (utterance[:, None] == piece_ids[None, :])[None]
        probability = jnp.exp(jnp.where(same_utt, scores - lse_local[:, :, None], NEGATIVE))
        dprobs = jnp.einsum(
            "qhd,khd->hqk", grad_heads, value_part, preferred_element_type=jnp.float32
        )
        dscores = (probability * (dprobs - delta_local[:, :, None])).astype(jnp.bfloat16)
        return running + jnp.einsum(
            "hqk,khd->hqd", dscores, key_part, preferred_element_type=jnp.float32
        )

    def key_side(running, pieces):
        query_piece, grad_piece, lse_up, lse_low, delta_up, delta_low, piece_ids = pieces
        piece_rows = query_piece.shape[0]
        query_part = query_piece.reshape(piece_rows, local_heads, HS)
        grad_part = grad_piece.reshape(piece_rows, local_heads, HS)
        lse_piece = joined(lse_up, lse_low).T
        delta_piece = joined(delta_up, delta_low).T
        key_total, value_total = running
        scores = (
            jnp.einsum("qhd,khd->hqk", query_part, key_heads, preferred_element_type=jnp.float32)
            * inv_root
        )
        same_utt = (piece_ids[:, None] == utterance[None, :])[None]
        probability = jnp.exp(jnp.where(same_utt, scores - lse_piece[:, :, None], NEGATIVE))
        value_total = value_total + jnp.einsum(
            "hqk,qhd->hkd",
            probability.astype(jnp.bfloat16),
            grad_part,
            preferred_element_type=jnp.float32,
        )
        dprobs = jnp.einsum(
            "qhd,khd->hqk", grad_part, value_heads, preferred_element_type=jnp.float32
        )
        dscores = (probability * (dprobs - delta_piece[:, :, None])).astype(jnp.bfloat16)
        key_total = key_total + jnp.einsum(
            "hqk,qhd->hkd", dscores, query_part, preferred_element_type=jnp.float32
        )
        return (key_total, value_total)

    query_total = by_blocks(
        query_side,
        empty_heads,
        (
            lax.all_gather(keys, "ctx", axis=0, tiled=True),
            lax.all_gather(values, "ctx", axis=0, tiled=True),
            lax.all_gather(utterance, "ctx", axis=0, tiled=True),
        ),
    )
    key_total, value_total = by_blocks(
        key_side,
        (empty_heads, empty_heads),
        (
            lax.all_gather(queries, "ctx", axis=0, tiled=True),
            lax.all_gather(attn_grad, "ctx", axis=0, tiled=True),
            lax.all_gather(lse_upper, "ctx", axis=0, tiled=True),
            lax.all_gather(lse_lower, "ctx", axis=0, tiled=True),
            lax.all_gather(delta_upper, "ctx", axis=0, tiled=True),
            lax.all_gather(delta_lower, "ctx", axis=0, tiled=True),
            lax.all_gather(utterance, "ctx", axis=0, tiled=True),
        ),
    )

    def to_frames(stacked, factor):
        return (
            (stacked * factor)
            .transpose(1, 0, 2)
            .reshape(frame_count, local_heads * HS)
            .astype(jnp.bfloat16)
        )

    return (
        output,
        to_frames(query_total, inv_root),
        to_frames(key_total, inv_root),
        to_frames(value_total, 1.0),
    )


def solution(mesh):
    placed = (
        P("ctx", "tp"),
        P("ctx", "tp"),
        P("ctx", "tp"),
        P("ctx"),
        P("tp", None),
        P("ctx", "tp"),
    )
    return jax.shard_map(
        shards,
        mesh=mesh,
        in_specs=placed,
        out_specs=(P("ctx", "tp"), P("ctx", "tp"), P("ctx", "tp"), P("ctx", "tp")),
        check_vma=False,
    )
```

profile of v0, /device:TPU:0, one launch (start us, length us, event | category | flops | bytes accessed | tf_op | source)
XLA Modules:
  0.0 280.9 jit_solution(10671385922212492002)
XLA Ops:
  7.3 8.3 %all_gather.37 = bf16[128,1536]{1,0:T(8,128)(2,1)S(1)} all-gather(bf16[128,384]{1,0:T(8,128)(2,1)} %param.17), channel_id=1, replica_groups=mesh['ctx'=8,'tp'=4] {'tp'}, dimensions={1}, use_global_device_ids=true | all-gather | bytes 491520 | tf_op jit(solution)/shard_map/all_gather | solution.py:85
  16.1 0.7 copy-done.8
  16.7 20.7 %all-gather = s32[8,1,128]{2,1,0:T(1,128)S(1)} all-gather(s32[1,1,128]{2,1,0:T(1,128)S(1)} %bitcast.168), channel_id=1, replica_groups=mesh['ctx'=8,'tp'=4] {'ctx'}, dimensions={0}, use_global_device_ids=true | all-gather | bytes 4608 | tf_op jit(solution)/shard_map/all_gather | solution.py:76
  37.4 0.5 broadcast.132
  37.9 0.7 reduce.3
  38.6 31.3 %all_gather.35 = bf16[1024,256]{1,0:T(8,128)(2,1)S(1)} all-gather(bf16[128,256]{1,0:T(8,128)(2,1)S(1)} %copy-done.6), channel_id=1, replica_groups=mesh['ctx'=8,'tp'=4] {'ctx'}, dimensions={0}, use_global_device_ids=true | all-gather | bytes 589824 | tf_op jit(solution)/shard_map/all_gather | solution.py:74
  70.1 0.6 copy-done.5
  70.8 0.7 copy-done.7
  71.6 31.3 %all_gather.36 = bf16[1024,256]{1,0:T(8,128)(2,1)S(1)} all-gather(bf16[128,256]{1,0:T(8,128)(2,1)S(1)} %copy-done.7), channel_id=1, replica_groups=mesh['ctx'=8,'tp'=4] {'ctx'}, dimensions={0}, use_global_device_ids=true | all-gather | bytes 589824 | tf_op jit(solution)/shard_map/all_gather | solution.py:75
  102.9 1.0 copy.54
  103.9 4.3 %while.39 = (s32[]{:T(128)}, f32[4,128]{1,0:T(4,128)S(1)}, f32[4,128]{1,0:T(4,128)S(1)}, f32[4,128,64]{1,2,0:T(8,128)S(1)}, s32[128]{0:T(128)S(1)}, /*index=5*/s...) while((s32[]{:T(128)}, f32[4,128]{1,0:T(4,128)S(1)}, ...), condition=%wide.region_3.4_spmd.clone, body=%wide.region_0.3_spmd.clone.sunk | while | flops 69634560 | bytes 5347977 | solution.py:31
  103.9 1.0 constant_dynamic-slice_fusion.15
  106.1 1.0 constant_dynamic-slice_fusion.15
  108.3 0.6 copy-done.3
  109.1 0.9 copy.67
  110.1 33.5 %all_gather.38 = bf16[1024,256]{1,0:T(8,128)(2,1)} all-gather(bf16[128,256]{1,0:T(8,128)(2,1)S(1)} %copy-done.5), channel_id=1, replica_groups=mesh['ctx'=8,'tp'=4] {'ctx'}, dimensions={0}, use_global_device_ids=true | all-gather | bytes 589824 | tf_op jit(solution)/shard_map/all_gather | solution.py:161
  143.6 0.7 copy.58
  144.4 17.4 %all_gather.39 = bf16[1024,4]{0,1:T(4,128)(2,1)} all-gather(bf16[128,4]{0,1:T(4,128)(2,1)S(1)} %bitcast_convert_fusion), channel_id=1, replica_groups=mesh['ctx'=8,'tp'=4] {'ctx'}, dimensions={0}, use_global_device_ids=true | all-gather | bytes 9216 | tf_op jit(solution)/shard_map/all_gather | solution.py:163
  161.8 33.2 %all_gather.41 = bf16[1024,256]{1,0:T(8,128)(2,1)} all-gather(bf16[128,256]{1,0:T(8,128)(2,1)S(1)} %convolution_convert_fusion.1), channel_id=1, replica_groups=mesh['ctx'=8,'tp'=4] {'ctx'}, dimensions={0}, use_global_device_ids=true | all-gather | bytes 589824 | tf_op jit(solution)/shard_map/all_gather | solution.py:162
  195.0 0.7 copy.59
  195.7 19.1 %all_gather.42 = bf16[1024,4]{0,1:T(4,128)(2,1)} all-gather(bf16[128,4]{0,1:T(4,128)(2,1)S(1)} %convert_element_type.121), channel_id=1, replica_groups=mesh['ctx'=8,'tp'=4] {'ctx'}, dimensions={0}, use_global_device_ids=true | all-gather | bytes 9216 | tf_op jit(solution)/shard_map/all_gather | solution.py:165
  214.8 0.6 add_bitcast_fusion.3
  215.4 0.6 add_bitcast_fusion.2
  216.0 17.3 %all_gather.40 = bf16[1024,4]{0,1:T(4,128)(2,1)} all-gather(bf16[128,4]{0,1:T(4,128)(2,1)S(1)} %get-tuple-element.485), channel_id=1, replica_groups=mesh['ctx'=8,'tp'=4] {'ctx'}, dimensions={0}, use_global_device_ids=true | all-gather | bytes 9216 | tf_op jit(solution)/shard_map/all_gather | solution.py:164
  233.3 19.1 %all_gather.43 = bf16[1024,4]{0,1:T(4,128)(2,1)} all-gather(bf16[128,4]{0,1:T(4,128)(2,1)S(1)} %get-tuple-element.481), channel_id=1, replica_groups=mesh['ctx'=8,'tp'=4] {'ctx'}, dimensions={0}, use_global_device_ids=true | all-gather | bytes 9216 | tf_op jit(solution)/shard_map/all_gather | solution.py:166
  252.3 10.7 %while.41 = (s32[]{:T(128)}, f32[4,128,64]{1,2,0:T(8,128)S(1)}, f32[4,128,64]{1,2,0:T(8,128)S(1)}, s32[2,512]{1,0:T(2,128)S(1)}, s32[128]{0:T(128)S(1)}, /*index...) while((s32[]{:T(128)}, f32[4,128,64]{1,2,0:T(8,128)S(1)}, ...), condition=%wide.region_9.10_spmd.clone, body=%wide.region_8.9_spmd.clone.sunk | while | flops 136261632 | bytes 7133868 | solution.py:31
  252.3 1.1 constant_dynamic-slice_fusion.19
  253.5 0.7 add_bitcast_fusion.5
  254.4 1.4 fusion.94
  255.9 1.5 fusion.95
  257.7 1.1 constant_dynamic-slice_fusion.19
  258.9 0.7 add_bitcast_fusion.5
  259.8 1.4 fusion.94
  261.3 1.5 fusion.95
  263.1 0.7 copy-done.9
  263.7 6.4 %while.40 = (s32[]{:T(128)}, f32[4,128,64]{1,2,0:T(8,128)S(1)}, s32[128]{0:T(128)S(1)}, s32[2,512]{1,0:T(2,128)S(1)}, bf16[2,512,256]{1,2,0:T(8,128)(2,1)S(1)}, ...) while((s32[]{:T(128)}, f32[4,128,64]{1,2,0:T(8,128)S(1)}, ...), condition=%wide.region_7.8_spmd.clone, body=%wide.region_6.7_spmd.clone.sunk | while | flops 102367232 | bytes 4999907 | solution.py:31
  263.7 1.0 constant_dynamic-slice_fusion.17
  264.9 0.7 copy-done.4
  265.6 0.4 fusion.85
  266.4 0.5 fusion.86
  266.9 1.0 constant_dynamic-slice_fusion.17
  268.1 0.7 copy-done.4
  268.8 0.4 fusion.85
  269.6 0.5 fusion.86
  270.2 0.7 copy.62
  270.9 0.7 copy.63
  271.7 0.7 copy.64
  272.4 1.6 copy.68
  (72 shorter events, 5.9 us)
Async XLA Ops:
  7.2 8.4 %copy-start = (bf16[256,1536]{1,0:T(8,128)(2,1)S(1)}, bf16[256,1536]{1,0:T(8,128)(2,1)}, u32[]{:S(2)}) copy-start(bf16[256,1536]{1,0:T(8,128)(2,1)} %param.16) | copy-start | bytes 2359300
  7.2 265.3 %reduce-scatter.4.cloned.1.call-start = ((), (), s32[]{:S(2)}) async-start(), calls=%async_computation.1 | async-start | bytes 491520
  15.9 22.7 %copy-start.6 = (bf16[128,256]{1,0:T(8,128)(2,1)S(1)}, bf16[128,256]{1,0:T(8,128)(2,1)}, u32[]{:S(2)}) copy-start(bf16[128,256]{1,0:T(8,128)(2,1)} %param.13) | copy-start | bytes 196612
  16.1 92.2 %copy-start.1 = (bf16[128,256]{0,1:T(8,128)(2,1)}, bf16[128,256]{0,1:T(8,128)(2,1)S(1)}, u32[]{:S(2)}) copy-start(bf16[128,256]{0,1:T(8,128)(2,1)S(1)} %copy.55) | copy-start | bytes 196612
  16.1 0.7 copy-start.8
  69.9 0.8 copy-start.5
  70.7 0.8 copy-start.7
  108.2 0.6 copy-start.3
  263.0 0.7 copy-start.9
  264.7 0.8 copy-start.4
  264.8 0.8 copy-start.10
  265.6 0.8 copy-start.2
  268.0 0.8 copy-start.4
  268.0 0.8 copy-start.10
  268.8 0.8 copy-start.2
Sparse Core Ops, SparseCore 0:
  110.2 17.7 reduce-scatter.3
where the time goes:
time: 282 us; the launch traced here: 281 us
  blocking collectives  231 us (82%)
  local copies, waits for them, and re-layouts  20.4 us (7%)
  between operations  14.2 us (5%)
  matrix products  10.1 us (4%)
  other arithmetic  4.64 us (2%)
    all_gather x1, blocking collectives, shards(): lax.all_gather(queries, 'ctx', axis=0, tiled=True)  33.5 us
    all_gather x1, blocking collectives, shards(): lax.all_gather(attn_grad, 'ctx', axis=0, tiled=True)  33.2 us
    all_gather x1, blocking collectives, shards(): lax.all_gather(values, 'ctx', axis=0, tiled=True)  31.3 us
    all_gather x1, blocking collectives, shards(): lax.all_gather(keys, 'ctx', axis=0, tiled=True)  31.3 us
    all_gather x1, blocking collectives, shards(): lax.all_gather(utterance, 'ctx', axis=0, tiled=True)  20.7 us
    all_gather x1, blocking collectives, shards(): lax.all_gather(delta_lower, 'ctx', axis=0, tiled=True)  19.1 us
    all_gather x1, blocking collectives, shards(): lax.all_gather(delta_upper, 'ctx', axis=0, tiled=True)  19.1 us
    all_gather x1, blocking collectives, shards(): lax.all_gather(lse_upper, 'ctx', axis=0, tiled=True)  17.4 us
  transfers between devices with their start and end apart: 1, of which 0 were waited for; matrix products, arithmetic and copies ran while one was open for 7% of the time, Pallas kernels for 0%

commit v1 on v0

v1 whole, which is shorter than its diff:
```python
import functools
import math

import jax
import jax.numpy as jnp
from jax import lax
from jax.experimental import pallas as pl
from jax.experimental.pallas import tpu as pltpu
from jax.sharding import PartitionSpec as P

HS = 64
SLOTS = 16
APART = 131072.0
MESH = pl.DeviceIdType.MESH
F32 = jnp.float32
BF16 = jnp.bfloat16


def loop(low, high, body, carry):
    if high - low <= 1:
        for i in range(low, high):
            carry = body(i, carry)
        return carry
    return lax.fori_loop(low, high, body, carry)


def dot_nn(a, b):
    return jnp.dot(a, b, preferred_element_type=F32)


def dot_nt(a, b):
    return lax.dot_general(a, b, (((1,), (1,)), ((), ())), preferred_element_type=F32)


def turned(x):
    return jnp.transpose(x.astype(F32)).astype(BF16)


def remote(src, dst, send, recv, device):
    return pltpu.make_async_remote_copy(
        src_ref=src, dst_ref=dst, send_sem=send, recv_sem=recv, device_id=device, device_id_type=MESH
    )


def kernel(
    dims,
    q_in, k_in, v_in, u_ref, w_in, c_in,
    out_ref, dq_ref, dk_ref, dv_ref,
    q_v, k_v, v_v, w_v, cot,
    kv_snd, kv_all, kv_turn, q_snd, q_rcv, do_snd, do_rcv, o_snd, o_rcv, dq_snd, dq_rcv,
    grid, own, part_snd, part_rcv, fin_snd, fin_rcv, rs_snd, rs_rcv,
    local_sem, kv_s, kv_r, q_s, q_r, do_s, do_r, o_s, o_r, dq_s, dq_r, fin_s, fin_r,
    row_s, row_r, part_s, part_r, cot_s, cot_r, rs_s, rs_r,
):
    H, G, T, F = dims
    c = lax.axis_index("ctx")
    t = lax.axis_index("tp")
    h = c // G
    g = lax.rem(c, G)
    scale = HS ** (-0.5)
    expo = scale * math.log2(math.e)
    Q = H * F
    R = F * (2 if H % 2 == 0 else 1)

    loads = [
        pltpu.make_async_copy(src, dst, local_sem.at[i])
        for i, (src, dst) in enumerate(
            ((k_in, k_v), (v_in, v_v), (q_in, q_v), (c_in, cot.at[t]), (w_in, w_v))
        )
    ]
    for one in loads:
        one.start()

    def up(d):
        return lax.rem(h + d, H)

    def side(e):
        return lax.rem(g + e, G)

    def lane(f):
        return lax.rem(t + f, T)

    barrier = pltpu.get_barrier_semaphore()

    def greet(device):
        pl.semaphore_signal(barrier, inc=1, device_id=device, device_id_type=MESH)

    for d in range(1, H):
        greet((up(d) * G + g, t))

    def greet_side(e, carry):
        greet((h * G + side(e), t))
        return carry

    loop(1, G, greet_side, 0)
    for f in range(1, T):
        greet((c, lane(f)))

    same = (lax.broadcasted_iota(jnp.int32, (SLOTS, F), 0) == u_ref[...]).astype(F32).astype(BF16)
    loads[0].wait()
    loads[1].wait()
    keys, values = k_v[...], v_v[...]
    for i in range(H):
        cols = slice(i * HS, (i + 1) * HS)
        kv_snd[i, 0:F, :] = jnp.concatenate([keys[:, cols], values[:, cols]], axis=1)
        kv_snd[i, F:, :] = same
    loads[2].wait()
    q_turn = turned(q_v[...])
    for i in range(H):
        q_snd[i] = q_turn[i * HS:(i + 1) * HS, :]
    loads[3].wait()
    pl.semaphore_wait(barrier, (H - 1) + (G - 1) + (T - 1))

    def kv_copy(to, at):
        return remote(kv_snd.at[to], kv_all.at[g, at], kv_s.at[to], kv_r.at[at], (to * G + g, t))

    def column(snd, rcv, send, recv):
        def build(to, at):
            return remote(snd.at[to], rcv.at[at], send.at[to], recv.at[at], (to * G + g, t))
        return build

    q_copy = column(q_snd, q_rcv, q_s, q_r)
    do_copy = column(do_snd, do_rcv, do_s, do_r)
    o_copy = column(o_snd, o_rcv, o_s, o_r)
    dq_copy = column(dq_snd, dq_rcv, dq_s, dq_r)
    fin_copy = column(fin_snd, fin_rcv, fin_s, fin_r)

    def row_copy(to, at, block):
        return remote(
            kv_all.at[at, block], kv_all.at[at, block], row_s.at[to, block], row_r.at[at, block],
            (h * G + to, t),
        )

    def part_copy(to, at):
        return remote(part_snd.at[to], part_rcv.at[at], part_s.at[to], part_r.at[at], (h * G + to, t))

    def cot_copy(to, at):
        return remote(cot.at[at], cot.at[at], cot_s.at[to], cot_r.at[at], (c, to))

    def rs_copy(to, at):
        return remote(rs_snd.at[to], rs_rcv.at[at], rs_s.at[to], rs_r.at[at], (c, to))

    def send_column(build):
        for d in range(1, H):
            build(up(d), h).start()

    def wait_column(build):
        for d in range(1, H):
            build(up(d), up(d)).wait_recv()

    def sent_column(build):
        for d in range(1, H):
            build(up(d), h).wait_send()

    for d in range(1, H):
        kv_copy(up(d), h).start()
        q_copy(up(d), h).start()
    for f in range(1, T):
        cot_copy(lane(f), t).start()
    kv_all[g, h] = kv_snd[h]
    q_rcv[h] = q_snd[h]

    def forward(block):
        def step(e, carry):
            row_copy(side(e), g, block).start()
            return carry
        loop(1, G, step, 0)

    forward(h)
    for d in range(1, H):
        kv_copy(up(d), up(d)).wait_recv()
        forward(up(d))

    loads[4].wait()
    for f in range(1, T):
        cot_copy(lane(f), lane(f)).wait_recv()
    width = cot.shape[2]
    grad = dot_nt(w_v[:, 0:width], cot[0])
    for i in range(1, T):
        grad += dot_nt(w_v[:, i * width:(i + 1) * width], cot[i])
    grad = grad.astype(BF16)
    for i in range(H):
        do_snd[i] = grad[i * HS:(i + 1) * HS, :]
    send_column(do_copy)
    do_rcv[h] = do_snd[h]

    wait_column(q_copy)
    q_all = jnp.concatenate([q_rcv[i] for i in range(H)], axis=1)

    def away(i):
        hot = kv_all[g, i, F:, :].astype(F32)
        return ((hot - 1.0) * APART).astype(BF16)

    q_wide = jnp.concatenate([q_all, jnp.concatenate([away(i) for i in range(H)], axis=1)], axis=0)

    def score(at, top):
        for i in range(H):
            block = kv_all[at, i, 0:F, :]
            kv_turn[at, :, i * F:(i + 1) * F] = turned(block)
            hot = turned(kv_all[at, i, F:, :])
            wide = jnp.concatenate([block[:, 0:HS], hot], axis=1)
            s = dot_nn(wide, q_wide)
            grid[at, i * F:(i + 1) * F, :] = s
            top = jnp.maximum(top, jnp.max(s, axis=0, keepdims=True))
        return top

    top = score(g, jnp.full((1, Q), -jnp.inf, F32))

    def score_side(e, top):
        at = side(e)
        for i in range(H):
            row_copy(at, at, i).wait_recv()
        return score(at, top)

    top = loop(1, G, score_side, top)

    def mix(at, carry):
        total, mixed = carry
        for r in range(0, Q, R):
            w = jnp.exp2((grid[at, r:r + R, :] - top) * expo)
            grid[at, r:r + R, :] = w
            total = total + jnp.sum(w, axis=0, keepdims=True)
            mixed = mixed + dot_nn(kv_turn[at, HS:, r:r + R], w.astype(BF16))
        return total, mixed

    total, mixed = loop(0, G, mix, (jnp.zeros((1, Q), F32), jnp.zeros((HS, Q), F32)))
    inverse = 1.0 / total
    attn = (mixed * inverse).astype(BF16)
    for i in range(H):
        o_snd[i] = attn[:, i * F:(i + 1) * F]
    send_column(o_copy)
    o_rcv[h] = o_snd[h]

    wait_column(do_copy)
    do_all = jnp.concatenate([do_rcv[i] for i in range(H)], axis=1)
    delta = jnp.sum(do_all.astype(F32) * attn.astype(F32), axis=0, keepdims=True)

    def back(at, r):
        p = grid[at, r:r + R, :] * inverse
        dv = dot_nt(p.astype(BF16), do_all)
        rows = [kv_all[at, i, 0:F, HS:] for i in range(r // F, (r + R) // F)]
        dp = dot_nn(jnp.concatenate(rows, axis=0), do_all)
        ds = (p * (dp - delta)).astype(BF16)
        dk = dot_nt(ds, q_all) * scale
        dq = dot_nn(kv_turn[at, 0:HS, r:r + R], ds)
        return jnp.concatenate([dk, dv], axis=1), dq

    def back_side(e, query_total):
        at = side(e)
        for r in range(0, Q, R):
            part, dq = back(at, r)
            part_snd[at, r:r + R, :] = part.astype(BF16)
            query_total = query_total + dq
        part_copy(at, g).start()
        return query_total

    query_total = loop(1, G, back_side, jnp.zeros((HS, Q), F32))

    wait_column(o_copy)
    mine = turned(jnp.concatenate([o_rcv[i] for i in range(H)], axis=0))
    for i in range(T):
        rs_snd[i] = dot_nn(mine, w_v[:, i * width:(i + 1) * width]).astype(BF16)
    for f in range(1, T):
        rs_copy(lane(f), t).start()
    rs_rcv[t] = rs_snd[t]

    for r in range(0, Q, R):
        part, dq = back(g, r)
        own[r:r + R, :] = part
        query_total = query_total + dq
    query_out = (query_total * scale).astype(BF16)
    for i in range(H):
        dq_snd[i] = query_out[:, i * F:(i + 1) * F]
    send_column(dq_copy)
    dq_rcv[h] = dq_snd[h]

    def gather_part(e, carry):
        at = side(e)
        part_copy(at, at).wait_recv()
        own[...] += part_rcv[at].astype(F32)
        return carry

    loop(1, G, gather_part, 0)
    for i in range(H):
        fin_snd[i] = own[i * F:(i + 1) * F, :].astype(BF16)
    send_column(fin_copy)
    fin_rcv[h] = fin_snd[h]

    for f in range(1, T):
        rs_copy(lane(f), lane(f)).wait_recv()
    summed = rs_rcv[0].astype(F32)
    for i in range(1, T):
        summed += rs_rcv[i].astype(F32)
    out_ref[...] = summed.astype(BF16)

    wait_column(dq_copy)
    dq_ref[...] = turned(jnp.concatenate([dq_rcv[i] for i in range(H)], axis=0))
    wait_column(fin_copy)
    dk_ref[...] = jnp.concatenate([fin_rcv[i, :, 0:HS] for i in range(H)], axis=1)
    dv_ref[...] = jnp.concatenate([fin_rcv[i, :, HS:] for i in range(H)], axis=1)

    for build in (kv_copy, q_copy, do_copy, o_copy, dq_copy, fin_copy):
        sent_column(build)

    def sent_side(e, carry):
        for i in range(H):
            row_copy(side(e), g, i).wait_send()
        part_copy(side(e), g).wait_send()
        return carry

    loop(1, G, sent_side, 0)
    for f in range(1, T):
        cot_copy(lane(f), t).wait_send()
        rs_copy(lane(f), t).wait_send()


def solution(mesh):
    n, T = mesh.shape["ctx"], mesh.shape["tp"]

    def step(queries, keys, values, utterance, w_out, cotangent):
        F, columns = queries.shape
        H = columns // HS
        G = n // H
        D = w_out.shape[1]
        width = cotangent.shape[1]
        Q = H * F
        vm = pltpu.VMEM
        dma = pltpu.SemaphoreType.DMA
        shapes = [
            vm((F, columns), BF16), vm((F, columns), BF16), vm((F, columns), BF16), vm((columns, D), BF16),
            vm((T, F, width), BF16),
            vm((H, F + SLOTS, 2 * HS), BF16), vm((G, H, F + SLOTS, 2 * HS), BF16), vm((G, 2 * HS, Q), BF16),
            vm((H, HS, F), BF16), vm((H, HS, F), BF16), vm((H, HS, F), BF16), vm((H, HS, F), BF16),
            vm((H, HS, F), BF16), vm((H, HS, F), BF16), vm((H, HS, F), BF16), vm((H, HS, F), BF16),
            vm((G, Q, Q), F32), vm((Q, 2 * HS), F32),
            vm((G, Q, 2 * HS), BF16), vm((G, Q, 2 * HS), BF16),
            vm((H, F, 2 * HS), BF16), vm((H, F, 2 * HS), BF16),
            vm((T, F, width), BF16), vm((T, F, width), BF16),
            dma((5,)),
        ] + [dma((H,))] * 12 + [dma((G, H))] * 2 + [dma((G,))] * 2 + [dma((T,))] * 4
        whole = pl.BlockSpec(memory_space=pl.ANY)
        here = pl.BlockSpec(memory_space=pltpu.VMEM)
        return pl.pallas_call(
            functools.partial(kernel, (H, G, T, F)),
            out_shape=(
                jax.ShapeDtypeStruct((F, width), BF16),
                jax.ShapeDtypeStruct((F, columns), BF16),
                jax.ShapeDtypeStruct((F, columns), BF16),
                jax.ShapeDtypeStruct((F, columns), BF16),
            ),
            in_specs=[whole, whole, whole, here, whole, whole],
            out_specs=(here, here, here, here),
            scratch_shapes=shapes,
            compiler_params=pltpu.CompilerParams(
                collective_id=0, has_side_effects=True, vmem_limit_bytes=48 * 1024 * 1024
            ),
        )(queries, keys, values, utterance.reshape(1, F), w_out, cotangent)

    placed = (P("ctx", "tp"), P("ctx", "tp"), P("ctx", "tp"), P("ctx"), P("tp", None), P("ctx", "tp"))
    return jax.shard_map(
        step, mesh=mesh, in_specs=placed, out_specs=(P("ctx", "tp"),) * 4, check_vma=False
    )
```

time: 282 us -> 35.3 us (0.13)
  blocking collectives: 231 us -> 0 us
  Pallas kernels: 0 us -> 26.5 us
  between operations: 14.2 us -> 0.66 us
  local copies, waits for them, and re-layouts: 20.4 us -> 7.72 us
  matrix products: 10.1 us -> 0 us
  other arithmetic: 4.64 us -> 0 us
    all_gather x10 -> x0, blocking collectives: 231 us -> none  [the longest x1 33.5 us: shards(): lax.all_gather(queries, 'ctx', axis=0, tiled=True)]
    pallas_call x0 -> x1, Pallas kernels: none -> 26.5 us  [step(): pl.pallas_call(functools.partial(kernel, (H, G, T, F)), out_shape=(jax.Sh...]
    dot_general x16 -> x0, matrix products: 10.1 us -> none  [the longest x2 3.02 us: key_side(): jnp.einsum('hqk,qhd->hkd', dscores, query_part, preferred_element_type=jn...]
    dynamic_slice x16 -> x0, local copies, waits for them, and re-layouts: 6.8 us -> none  [by_blocks(): running, unused = lax.scan(one_turn, running, stacked)]
    unnamed x26 -> x16, local copies, waits for them, and re-layouts: 10.8 us -> 7.72 us
  transfers between devices with their start and end apart: 1 -> 0, of which waited for: 0 -> 0; matrix products, arithmetic and copies ran while one was open for 7% -> 0% of each run, Pallas kernels for 0% -> 0%
where the time goes in v1:
time: 35.3 us; the launch traced here: 34.9 us
  Pallas kernels  26.5 us (75%)
  local copies, waits for them, and re-layouts  7.72 us (22%)
  between operations  0.66 us (2%)
    pallas_call x1, Pallas kernels, step(): pl.pallas_call(functools.partial(kernel, (H, G, T, F)), out_shape=(jax.Sh...  26.5 us
    unnamed x16, local copies, waits for them, and re-layouts  7.72 us

profile of v1, /device:TPU:0, one launch (start us, length us, event | category | flops | bytes accessed | tf_op | source)
XLA Modules:
  0.0 34.9 jit_solution(9192618071719124165)
XLA Ops:
  0.6 0.0 copy-start.5
  0.6 0.6 %copy-done.5 = s32[128]{0:T(128)S(1)} copy-done((s32[128]{0:T(128)S(1)}, s32[128]{0:T(128)}, u32[]{:S(2)}) %copy-start.5) | copy-done | bytes 536
  1.3 0.0 copy-start
  1.3 1.1 %copy-done = bf16[256,1536]{1,0:T(8,128)(2,1)S(1)} copy-done((bf16[256,1536]{1,0:T(8,128)(2,1)S(1)}, bf16[256,1536]{1,0:T(8,128)(2,1)}, u32[]{:S(2)}) %copy-start) | copy-done | bytes 786456
  2.4 0.0 copy-start.1
  2.4 0.9 %copy-done.1 = bf16[128,384]{1,0:T(8,128)(2,1)S(1)} copy-done((bf16[128,384]{1,0:T(8,128)(2,1)S(1)}, bf16[128,384]{1,0:T(8,128)(2,1)}, u32[]{:S(2)}) %copy-start.1) | copy-done | bytes 98328
  3.3 0.0 copy-start.2
  3.3 0.8 %copy-done.2 = bf16[128,256]{1,0:T(8,128)(2,1)S(1)} copy-done((bf16[128,256]{1,0:T(8,128)(2,1)S(1)}, bf16[128,256]{1,0:T(8,128)(2,1)}, u32[]{:S(2)}) %copy-start.2) | copy-done | bytes 65560
  4.2 0.0 copy-start.3
  4.2 0.8 %copy-done.3 = bf16[128,256]{1,0:T(8,128)(2,1)S(1)} copy-done((bf16[128,256]{1,0:T(8,128)(2,1)S(1)}, bf16[128,256]{1,0:T(8,128)(2,1)}, u32[]{:S(2)}) %copy-start.3) | copy-done | bytes 65560
  5.0 0.0 copy-start.4
  5.0 0.8 %copy-done.4 = bf16[128,256]{1,0:T(8,128)(2,1)S(1)} copy-done((bf16[128,256]{1,0:T(8,128)(2,1)S(1)}, bf16[128,256]{1,0:T(8,128)(2,1)}, u32[]{:S(2)}) %copy-start.4) | copy-done | bytes 65560
  5.8 26.5 %shard_map.93 = (bf16[128,384]{1,0:T(8,128)(2,1)S(1)}, bf16[128,256]{1,0:T(8,128)(2,1)S(1)}, bf16[128,256]{1,0:T(8,128)(2,1)S(1)}, bf16[128,256]{1,0:T(8,128)(2,1)S(1)}) custom-call(bf16[128,256]{1,0:T(8,128)(2,1)S(1)} %copy-done.2, bf16[128,256]{1,0:T(8,128)(2,1)S(1)} %copy-done.3, bf16[128,256]{1,0:T(8,128)(2,1)S(1)} %copy-done.4, s32[1,128]{1,0:T(1,128)S(1)} %bitcast.1, ...), custom_call_target="tpu_custom_call" | custom-call | tf_op jit(solution)/shard_map/pallas_call | solution.py:343
  32.4 0.6 %copy.14 = bf16[128,384]{1,0:T(8,128)(2,1)} copy(bf16[128,384]{1,0:T(8,128)(2,1)S(1)} %get-tuple-element.8) | data formatting | bytes 196608
  33.0 0.6 %copy.15 = bf16[128,256]{1,0:T(8,128)(2,1)} copy(bf16[128,256]{1,0:T(8,128)(2,1)S(1)} %get-tuple-element.9) | data formatting | bytes 131072
  33.7 0.6 %copy.16 = bf16[128,256]{1,0:T(8,128)(2,1)} copy(bf16[128,256]{1,0:T(8,128)(2,1)S(1)} %get-tuple-element.10) | data formatting | bytes 131072
  34.3 0.6 %copy.17 = bf16[128,256]{1,0:T(8,128)(2,1)} copy(bf16[128,256]{1,0:T(8,128)(2,1)S(1)} %get-tuple-element.11) | data formatting | bytes 131072
Async XLA Ops:
  0.6 0.7 %copy-start.5 = (s32[128]{0:T(128)S(1)}, s32[128]{0:T(128)}, u32[]{:S(2)}) copy-start(s32[128]{0:T(128)} %param.9) | copy-start | bytes 1540
  1.3 1.1 %copy-start = (bf16[256,1536]{1,0:T(8,128)(2,1)S(1)}, bf16[256,1536]{1,0:T(8,128)(2,1)}, u32[]{:S(2)}) copy-start(bf16[256,1536]{1,0:T(8,128)(2,1)} %w_in.1) | copy-start | bytes 2359300
  2.4 0.9 %copy-start.1 = (bf16[128,384]{1,0:T(8,128)(2,1)S(1)}, bf16[128,384]{1,0:T(8,128)(2,1)}, u32[]{:S(2)}) copy-start(bf16[128,384]{1,0:T(8,128)(2,1)} %c_in.1) | copy-start | bytes 294916
  3.3 0.8 %copy-start.2 = (bf16[128,256]{1,0:T(8,128)(2,1)S(1)}, bf16[128,256]{1,0:T(8,128)(2,1)}, u32[]{:S(2)}) copy-start(bf16[128,256]{1,0:T(8,128)(2,1)} %q_in.1) | copy-start | bytes 196612
  4.2 0.8 %copy-start.3 = (bf16[128,256]{1,0:T(8,128)(2,1)S(1)}, bf16[128,256]{1,0:T(8,128)(2,1)}, u32[]{:S(2)}) copy-start(bf16[128,256]{1,0:T(8,128)(2,1)} %k_in.1) | copy-start | bytes 196612
  5.0 0.8 %copy-start.4 = (bf16[128,256]{1,0:T(8,128)(2,1)S(1)}, bf16[128,256]{1,0:T(8,128)(2,1)}, u32[]{:S(2)}) copy-start(bf16[128,256]{1,0:T(8,128)(2,1)} %v_in.1) | copy-start | bytes 196612

commit v2 on v1

--- a/solution.py
+++ b/solution.py
@@ -24,6 +24,12 @@
     return lax.fori_loop(low, high, body, carry)
 
 
+def pairs(items):
+    items = list(items)
+    step = 2 if len(items) % 2 == 0 else 1
+    return [items[i:i + step] for i in range(0, len(items), step)]
+
+
 def dot_nn(a, b):
     return jnp.dot(a, b, preferred_element_type=F32)
 
@@ -48,7 +54,7 @@
     out_ref, dq_ref, dk_ref, dv_ref,
     q_v, k_v, v_v, w_v, cot,
     kv_snd, kv_all, kv_turn, q_snd, q_rcv, do_snd, do_rcv, o_snd, o_rcv, dq_snd, dq_rcv,
-    grid, own, part_snd, part_rcv, fin_snd, fin_rcv, rs_snd, rs_rcv,
+    grid, tops, part_snd, part_rcv, fin_snd, fin_rcv, rs_snd, rs_rcv,
     local_sem, kv_s, kv_r, q_s, q_r, do_s, do_r, o_s, o_r, dq_s, dq_r, fin_s, fin_r,
     row_s, row_r, part_s, part_r, cot_s, cot_r, rs_s, rs_r,
 ):
@@ -60,7 +66,31 @@
     scale = HS ** (-0.5)
     expo = scale * math.log2(math.e)
     Q = H * F
-    R = F * (2 if H % 2 == 0 else 1)
+
+    def up(d):
+        return lax.rem(h + d, H)
+
+    def side(e):
+        return lax.rem(g + e, G)
+
+    def lane(f):
+        return lax.rem(t + f, T)
+
+    barrier = pltpu.get_barrier_semaphore()
+
+    def greet(device):
+        pl.semaphore_signal(barrier, inc=1, device_id=device, device_id_type=MESH)
+
+    for d in range(1, H):
+        greet((up(d) * G + g, t))
+
+    def greet_side(e, carry):
+        greet((h * G + side(e), t))
+        return carry
+
+    loop(1, G, greet_side, 0)
+    for f in range(1, T):
+        greet((c, lane(f)))
 
     loads = [
         pltpu.make_async_copy(src, dst, local_sem.at[i])
@@ -71,31 +101,6 @@
     for one in loads:
         one.start()
 
-    def up(d):
-        return lax.rem(h + d, H)
-
-    def side(e):
-        return lax.rem(g + e, G)
-
-    def lane(f):
-        return lax.rem(t + f, T)
-
-    barrier = pltpu.get_barrier_semaphore()
-
-    def greet(device):
-        pl.semaphore_signal(barrier, inc=1, device_id=device, device_id_type=MESH)
-
-    for d in range(1, H):
-        greet((up(d) * G + g, t))
-
-    def greet_side(e, carry):
-        greet((h * G + side(e), t))
-        return carry
-
-    loop(1, G, greet_side, 0)
-    for f in range(1, T):
-        greet((c, lane(f)))
-
     same = (lax.broadcasted_iota(jnp.int32, (SLOTS, F), 0) == u_ref[...]).astype(F32).astype(BF16)
     loads[0].wait()
     loads[1].wait()
@@ -131,8 +136,11 @@
             (h * G + to, t),
         )
 
-    def part_copy(to, at):
-        return remote(part_snd.at[to], part_rcv.at[at], part_s.at[to], part_r.at[at], (h * G + to, t))
+    def part_copy(to, at, block):
+        return remote(
+            part_snd.at[to, block], part_rcv.at[at, block], part_s.at[to, block], part_r.at[at, block],
+            (h * G + to, t),
+        )
 
     def cot_copy(to, at):
         return remote(cot.at[at], cot.at[at], cot_s.at[to], cot_r.at[at], (c, to))
@@ -145,7 +153,7 @@
             build(up(d), h).start()
 
     def wait_column(build):
-        for d in range(1, H):
+        for d in range(H - 1, 0, -1):
             build(up(d), up(d)).wait_recv()
 
     def sent_column(build):
@@ -167,7 +175,7 @@
         loop(1, G, step, 0)
 
     forward(h)
-    for d in range(1, H):
+    for d in range(H - 1, 0, -1):
         kv_copy(up(d), up(d)).wait_recv()
         forward(up(d))
 
@@ -193,37 +201,41 @@
 
     q_wide = jnp.concatenate([q_all, jnp.concatenate([away(i) for i in range(H)], axis=1)], axis=0)
 
-    def score(at, top):
+    def ahead(at):
+        top = None
         for i in range(H):
             block = kv_all[at, i, 0:F, :]
-            kv_turn[at, :, i * F:(i + 1) * F] = turned(block)
+            kv_turn[at, i] = turned(block)
             hot = turned(kv_all[at, i, F:, :])
             wide = jnp.concatenate([block[:, 0:HS], hot], axis=1)
             s = dot_nn(wide, q_wide)
-            grid[at, i * F:(i + 1) * F, :] = s
-            top = jnp.maximum(top, jnp.max(s, axis=0, keepdims=True))
-        return top
-
-    top = score(g, jnp.full((1, Q), -jnp.inf, F32))
-
-    def score_side(e, top):
+            grid[at, i] = s
+            here = jnp.max(s, axis=0, keepdims=True)
+            top = here if top is None else jnp.maximum(top, here)
+        tops[at] = top
+        total, mixed = jnp.zeros((1, Q), F32), jnp.zeros((HS, Q), F32)
+        for pair in pairs(range(H)):
+            parts = []
+            for i in pair:
+                w = jnp.exp2((grid[at, i] - top) * expo)
+                grid[at, i] = w
+                total = total + jnp.sum(w, axis=0, keepdims=True)
+                parts.append(w.astype(BF16))
+            lanes = jnp.concatenate([kv_turn[at, i, HS:, :] for i in pair], axis=1)
+            mixed = mixed + dot_nn(lanes, jnp.concatenate(parts, axis=0))
+        return top, total, mixed
+
+    def ahead_side(e, carry):
+        top, total, mixed = carry
         at = side(e)
         for i in range(H):
             row_copy(at, at, i).wait_recv()
-        return score(at, top)
-
-    top = loop(1, G, score_side, top)
-
-    def mix(at, carry):
-        total, mixed = carry
-        for r in range(0, Q, R):
-            w = jnp.exp2((grid[at, r:r + R, :] - top) * expo)
-            grid[at, r:r + R, :] = w
-            total = total + jnp.sum(w, axis=0, keepdims=True)
-            mixed = mixed + dot_nn(kv_turn[at, HS:, r:r + R], w.astype(BF16))
-        return total, mixed
-
-    total, mixed = loop(0, G, mix, (jnp.zeros((1, Q), F32), jnp.zeros((HS, Q), F32)))
+        new, more, other = ahead(at)
+        both = jnp.maximum(top, new)
+        old_part, new_part = jnp.exp2((top - both) * expo), jnp.exp2((new - both) * expo)
+        return both, total * old_part + more * new_part, mixed * old_part + other * new_part
+
+    top, total, mixed = loop(1, G, ahead_side, ahead(g))
     inverse = 1.0 / total
     attn = (mixed * inverse).astype(BF16)
     for i in range(H):
@@ -235,23 +247,26 @@
     do_all = jnp.concatenate([do_rcv[i] for i in range(H)], axis=1)
     delta = jnp.sum(do_all.astype(F32) * attn.astype(F32), axis=0, keepdims=True)
 
-    def back(at, r):
-        p = grid[at, r:r + R, :] * inverse
+    def back(at, pair):
+        factor = jnp.exp2((tops[at] - top) * expo) * inverse
+        p = jnp.concatenate([grid[at, b] for b in pair], axis=0) * factor
         dv = dot_nt(p.astype(BF16), do_all)
-        rows = [kv_all[at, i, 0:F, HS:] for i in range(r // F, (r + R) // F)]
-        dp = dot_nn(jnp.concatenate(rows, axis=0), do_all)
-        ds = (p * (dp - delta)).astype(BF16)
+        rows = jnp.concatenate([kv_all[at, b, 0:F, HS:] for b in pair], axis=0)
+        ds = (p * (dot_nn(rows, do_all) - delta)).astype(BF16)
         dk = dot_nt(ds, q_all) * scale
-        dq = dot_nn(kv_turn[at, 0:HS, r:r + R], ds)
+        dq = dot_nn(jnp.concatenate([kv_turn[at, b, 0:HS, :] for b in pair], axis=1), ds)
         return jnp.concatenate([dk, dv], axis=1), dq
+
+    order = [up(d) for d in range(1, H)] + [h]
 
     def back_side(e, query_total):
         at = side(e)
-        for r in range(0, Q, R):
-            part, dq = back(at, r)
-            part_snd[at, r:r + R, :] = part.astype(BF16)
+        for pair in pairs(order):
+            part, dq = back(at, pair)
+            for i, b in enumerate(pair):
+                part_snd[at, b] = part[i * F:(i + 1) * F, :].astype(BF16)
+                part_copy(at, g, b).start()
             query_total = query_total + dq
-        part_copy(at, g).start()
         return query_total
 
     query_total = loop(1, G, back_side, jnp.zeros((HS, Q), F32))
@@ -264,27 +279,27 @@
         rs_copy(lane(f), t).start()
     rs_rcv[t] = rs_snd[t]
 
-    for r in range(0, Q, R):
-        part, dq = back(g, r)
-        own[r:r + R, :] = part
+    def finish(b, part):
+        def gather(e, sofar):
+            at = side(e)
+            part_copy(at, at, b).wait_recv()
+            return sofar + part_rcv[at, b].astype(F32)
+
+        fin_snd[b] = loop(1, G, gather, part).astype(BF16)
+
+    for number, pair in enumerate(pairs(order)):
+        part, dq = back(g, pair)
         query_total = query_total + dq
+        for i, b in enumerate(pair):
+            finish(b, part[i * F:(i + 1) * F, :])
+            if number * len(pair) + i < H - 1:
+                fin_copy(b, h).start()
+    fin_rcv[h] = fin_snd[h]
     query_out = (query_total * scale).astype(BF16)
     for i in range(H):
         dq_snd[i] = query_out[:, i * F:(i + 1) * F]
     send_column(dq_copy)
     dq_rcv[h] = dq_snd[h]
-
-    def gather_part(e, carry):
-        at = side(e)
-        part_copy(at, at).wait_recv()
-        own[...] += part_rcv[at].astype(F32)
-        return carry
-
-    loop(1, G, gather_part, 0)
-    for i in range(H):
-        fin_snd[i] = own[i * F:(i + 1) * F, :].astype(BF16)
-    send_column(fin_copy)
-    fin_rcv[h] = fin_snd[h]
 
     for f in range(1, T):
         rs_copy(lane(f), lane(f)).wait_recv()
@@ -305,13 +320,24 @@
     def sent_side(e, carry):
         for i in range(H):
             row_copy(side(e), g, i).wait_send()
-        part_copy(side(e), g).wait_send()
+            part_copy(side(e), g, i).wait_send()
         return carry
 
     loop(1, G, sent_side, 0)
     for f in range(1, T):
         cot_copy(lane(f), t).wait_send()
         rs_copy(lane(f), t).wait_send()
+
+
+def store(a, b, c, d, a_out, b_out, c_out, d_out, sem):
+    moves = [
+        pltpu.make_async_copy(src, dst, sem.at[i])
+        for i, (src, dst) in enumerate(((a, a_out), (b, b_out), (c, c_out), (d, d_out)))
+    ]
+    for one in moves:
+        one.start()
+    for one in moves:
+        one.wait()
 
 
 def solution(mesh):
@@ -329,18 +355,18 @@
         shapes = [
             vm((F, columns), BF16), vm((F, columns), BF16), vm((F, columns), BF16), vm((columns, D), BF16),
             vm((T, F, width), BF16),
-            vm((H, F + SLOTS, 2 * HS), BF16), vm((G, H, F + SLOTS, 2 * HS), BF16), vm((G, 2 * HS, Q), BF16),
+            vm((H, F + SLOTS, 2 * HS), BF16), vm((G, H, F + SLOTS, 2 * HS), BF16), vm((G, H, 2 * HS, F), BF16),
             vm((H, HS, F), BF16), vm((H, HS, F), BF16), vm((H, HS, F), BF16), vm((H, HS, F), BF16),
             vm((H, HS, F), BF16), vm((H, HS, F), BF16), vm((H, HS, F), BF16), vm((H, HS, F), BF16),
-            vm((G, Q, Q), F32), vm((Q, 2 * HS), F32),
-            vm((G, Q, 2 * HS), BF16), vm((G, Q, 2 * HS), BF16),
+            vm((G, H, F, Q), F32), vm((G, 1, Q), F32),
+            vm((G, H, F, 2 * HS), BF16), vm((G, H, F, 2 * HS), BF16),
             vm((H, F, 2 * HS), BF16), vm((H, F, 2 * HS), BF16),
             vm((T, F, width), BF16), vm((T, F, width), BF16),
             dma((5,)),
-        ] + [dma((H,))] * 12 + [dma((G, H))] * 2 + [dma((G,))] * 2 + [dma((T,))] * 4
-        whole = pl.BlockSpec(memory_space=pl.ANY)
+        ] + [dma((H,))] * 12 + [dma((G, H))] * 4 + [dma((T,))] * 4
+        whole = pl.BlockSpec(memory_space=pltpu.HBM)
         here = pl.BlockSpec(memory_space=pltpu.VMEM)
-        return pl.pallas_call(
+        made = pl.pallas_call(
             functools.partial(kernel, (H, G, T, F)),
             out_shape=(
                 jax.ShapeDtypeStruct((F, width), BF16),
@@ -352,9 +378,16 @@
             out_specs=(here, here, here, here),
             scratch_shapes=shapes,
             compiler_params=pltpu.CompilerParams(
-                collective_id=0, has_side_effects=True, vmem_limit_bytes=48 * 1024 * 1024
+                collective_id=0, has_side_effects=True, vmem_limit_bytes=62 * 1024 * 1024
             ),
         )(queries, keys, values, utterance.reshape(1, F), w_out, cotangent)
+        return pl.pallas_call(
+            store,
+            out_shape=tuple(jax.ShapeDtypeStruct(x.shape, x.dtype) for x in made),
+            in_specs=[whole] * 4,
+            out_specs=(whole,) * 4,
+            scratch_shapes=[dma((4,))],
+        )(*made)
 
     placed = (P("ctx", "tp"), P("ctx", "tp"), P("ctx", "tp"), P("ctx"), P("tp", None), P("ctx", "tp"))
     return jax.shard_map(

time: 35.3 us -> 38.2 us (1.082)
  Pallas kernels: 26.5 us -> 37.4 us
  local copies, waits for them, and re-layouts: 7.72 us -> 0 us
    pallas_call x0 -> x1, Pallas kernels: none -> 10.1 us  [step(): pl.pallas_call(store, out_shape=tuple((jax.ShapeDtypeStruct(x.shape, x.dt...]
    unnamed x16 -> x0, local copies, waits for them, and re-layouts: 7.72 us -> none
    pallas_call x1, Pallas kernels: 26.5 us -> 27.3 us  [step(): pl.pallas_call(functools.partial(kernel, (H, G, T, F)), out_shape=(jax.Sh...]
where the time goes in v2:
time: 38.2 us; the launch traced here: 38.1 us
  Pallas kernels  37.4 us (98%)
  between operations  0.64 us (2%)
    pallas_call x1, Pallas kernels, step(): pl.pallas_call(functools.partial(kernel, (H, G, T, F)), out_shape=(jax.Sh...  27.3 us
    pallas_call x1, Pallas kernels, step(): pl.pallas_call(store, out_shape=tuple((jax.ShapeDtypeStruct(x.shape, x.dt...  10.1 us

profile of v2, /device:TPU:0, one launch (start us, length us, event | category | flops | bytes accessed | tf_op | source)
XLA Modules:
  0.0 38.1 jit_solution(12909669009179830615)
XLA Ops:
  0.6 27.3 %shard_map.93 = (bf16[128,384]{1,0:T(8,128)(2,1)}, bf16[128,256]{1,0:T(8,128)(2,1)}, bf16[128,256]{1,0:T(8,128)(2,1)}, bf16[128,256]{1,0:T(8,128)(2,1)}) custom-call(bf16[128,256]{1,0:T(8,128)(2,1)} %q_in.1, bf16[128,256]{1,0:T(8,128)(2,1)} %k_in.1, bf16[128,256]{1,0:T(8,128)(2,1)} %v_in.1, s32[1,128]{1,0:T(1,128)} %bitcast.1, bf16[256,1536]{1,0:T(8,128)(2,1)} %w_in.1, ...), custom_call_target="tpu_custom_call" | custom-call | tf_op jit(solution)/shard_map/pallas_call | solution.py:369
  28.0 10.1 %shard_map.94 = (bf16[128,384]{1,0:T(8,128)(2,1)}, bf16[128,256]{1,0:T(8,128)(2,1)}, bf16[128,256]{1,0:T(8,128)(2,1)}, bf16[128,256]{1,0:T(8,128)(2,1)}) custom-call(bf16[128,384]{1,0:T(8,128)(2,1)} %get-tuple-element.8.a, bf16[128,256]{1,0:T(8,128)(2,1)} %get-tuple-element.9.b, bf16[128,256]{1,0:T(8,128)(2,1)} %get-tuple-element.10.c, ...), custom_call_target="tpu_custom_call" | custom-call | tf_op jit(solution)/shard_map/pallas_call | solution.py:384

commit v3 on v2

--- a/solution.py
+++ b/solution.py
@@ -50,9 +50,9 @@
 
 def kernel(
     dims,
-    q_in, k_in, v_in, u_ref, w_in, c_in,
+    q_in, k_in, v_in, u_in, w_in, c_in,
     out_ref, dq_ref, dk_ref, dv_ref,
-    q_v, k_v, v_v, w_v, cot,
+    q_v, k_v, v_v, u_v, w_v, cot,
     kv_snd, kv_all, kv_turn, q_snd, q_rcv, do_snd, do_rcv, o_snd, o_rcv, dq_snd, dq_rcv,
     grid, tops, part_snd, part_rcv, fin_snd, fin_rcv, rs_snd, rs_rcv,
     local_sem, kv_s, kv_r, q_s, q_r, do_s, do_r, o_s, o_r, dq_s, dq_r, fin_s, fin_r,
@@ -95,13 +95,14 @@
     loads = [
         pltpu.make_async_copy(src, dst, local_sem.at[i])
         for i, (src, dst) in enumerate(
-            ((k_in, k_v), (v_in, v_v), (q_in, q_v), (c_in, cot.at[t]), (w_in, w_v))
+            ((k_in, k_v), (v_in, v_v), (q_in, q_v), (c_in, cot.at[t]), (w_in, w_v), (u_in, u_v))
         )
     ]
     for one in loads:
         one.start()
 
-    same = (lax.broadcasted_iota(jnp.int32, (SLOTS, F), 0) == u_ref[...]).astype(F32).astype(BF16)
+    loads[5].wait()
+    same = (lax.broadcasted_iota(jnp.int32, (SLOTS, F), 0) == u_v[...]).astype(F32).astype(BF16)
     loads[0].wait()
     loads[1].wait()
     keys, values = k_v[...], v_v[...]
@@ -353,7 +354,8 @@
         vm = pltpu.VMEM
         dma = pltpu.SemaphoreType.DMA
         shapes = [
-            vm((F, columns), BF16), vm((F, columns), BF16), vm((F, columns), BF16), vm((columns, D), BF16),
+            vm((F, columns), BF16), vm((F, columns), BF16), vm((F, columns), BF16),
+            vm((1, F), jnp.int32), vm((columns, D), BF16),
             vm((T, F, width), BF16),
             vm((H, F + SLOTS, 2 * HS), BF16), vm((G, H, F + SLOTS, 2 * HS), BF16), vm((G, H, 2 * HS, F), BF16),
             vm((H, HS, F), BF16), vm((H, HS, F), BF16), vm((H, HS, F), BF16), vm((H, HS, F), BF16),
@@ -362,10 +364,13 @@
             vm((G, H, F, 2 * HS), BF16), vm((G, H, F, 2 * HS), BF16),
             vm((H, F, 2 * HS), BF16), vm((H, F, 2 * HS), BF16),
             vm((T, F, width), BF16), vm((T, F, width), BF16),
-            dma((5,)),
+            dma((6,)),
         ] + [dma((H,))] * 12 + [dma((G, H))] * 4 + [dma((T,))] * 4
         whole = pl.BlockSpec(memory_space=pltpu.HBM)
         here = pl.BlockSpec(memory_space=pltpu.VMEM)
+        def pin(x):
+            return pltpu.with_memory_space_constraint(x, pltpu.HBM)
+
         made = pl.pallas_call(
             functools.partial(kernel, (H, G, T, F)),
             out_shape=(
@@ -374,19 +379,20 @@
                 jax.ShapeDtypeStruct((F, columns), BF16),
                 jax.ShapeDtypeStruct((F, columns), BF16),
             ),
-            in_specs=[whole, whole, whole, here, whole, whole],
+            in_specs=[whole] * 6,
             out_specs=(here, here, here, here),
             scratch_shapes=shapes,
             compiler_params=pltpu.CompilerParams(
-                collective_id=0, has_side_effects=True, vmem_limit_bytes=62 * 1024 * 1024
+                collective_id=0, has_side_effects=True, vmem_limit_bytes=48 * 1024 * 1024
             ),
-        )(queries, keys, values, utterance.reshape(1, F), w_out, cotangent)
+        )(pin(queries), pin(keys), pin(values), pin(utterance.reshape(1, F)), pin(w_out), pin(cotangent))
         return pl.pallas_call(
             store,
             out_shape=tuple(jax.ShapeDtypeStruct(x.shape, x.dtype) for x in made),
-            in_specs=[whole] * 4,
+            in_specs=[here] * 4,
             out_specs=(whole,) * 4,
             scratch_shapes=[dma((4,))],
+            compiler_params=pltpu.CompilerParams(vmem_limit_bytes=2 * 1024 * 1024),
         )(*made)
 
     placed = (P("ctx", "tp"), P("ctx", "tp"), P("ctx", "tp"), P("ctx"), P("tp", None), P("ctx", "tp"))

time: 38.2 us -> 27.6 us (0.72)
  Pallas kernels: 37.4 us -> 26.8 us
    pallas_call x1, Pallas kernels: 10.1 us -> 0.74 us  [step(): pl.pallas_call(store, out_shape=tuple((jax.ShapeDtypeStruct(x.shape, x.dt...]
    pallas_call x1, Pallas kernels: 27.3 us -> 26 us  [step(): pl.pallas_call(functools.partial(kernel, (H, G, T, F)), out_shape=(jax.Sh...]
where the time goes in v3:
time: 27.6 us; the launch traced here: 27.4 us
  Pallas kernels  26.8 us (97%)
  between operations  0.64 us (2%)
    pallas_call x1, Pallas kernels, step(): pl.pallas_call(functools.partial(kernel, (H, G, T, F)), out_shape=(jax.Sh...  26 us
    pallas_call x1, Pallas kernels, step(): pl.pallas_call(store, out_shape=tuple((jax.ShapeDtypeStruct(x.shape, x.dt...  0.74 us

profile of v3, /device:TPU:0, one launch (start us, length us, event | category | flops | bytes accessed | tf_op | source)
XLA Modules:
  0.0 27.4 jit_solution(7976558401179392919)
XLA Ops:
  0.6 26.0 %shard_map.93 = (bf16[128,384]{1,0:T(8,128)(2,1)S(1)}, bf16[128,256]{1,0:T(8,128)(2,1)S(1)}, bf16[128,256]{1,0:T(8,128)(2,1)S(1)}, bf16[128,256]{1,0:T(8,128)(2,1)S(1)}) custom-call(bf16[128,256]{1,0:T(8,128)(2,1)} %q_in.1, bf16[128,256]{1,0:T(8,128)(2,1)} %k_in.1, bf16[128,256]{1,0:T(8,128)(2,1)} %v_in.1, s32[1,128]{1,0:T(1,128)} %bitcast.1, ...), custom_call_target="tpu_custom_call" | custom-call | tf_op jit(solution)/shard_map/pallas_call | solution.py:374
  26.7 0.7 %shard_map.94 = (bf16[128,384]{1,0:T(8,128)(2,1)}, bf16[128,256]{1,0:T(8,128)(2,1)}, bf16[128,256]{1,0:T(8,128)(2,1)}, bf16[128,256]{1,0:T(8,128)(2,1)}) custom-call(bf16[128,384]{1,0:T(8,128)(2,1)S(1)} %get-tuple-element.8.a, bf16[128,256]{1,0:T(8,128)(2,1)S(1)} %get-tuple-element.9.b, bf16[128,256]{1,0:T(8,128)(2,1)S(1)} %get-tuple-element.10.c, ...), custom_call_target="tpu_custom_call" | custom-call | tf_op jit(solution)/shard_map/pallas_call | solution.py:389

commit v4 on v3

--- a/solution.py
+++ b/solution.py
@@ -143,8 +143,8 @@
             (h * G + to, t),
         )
 
-    def cot_copy(to, at):
-        return remote(cot.at[at], cot.at[at], cot_s.at[to], cot_r.at[at], (c, to))
+    def cot_copy(to, at, turn):
+        return remote(cot.at[at], cot.at[at], cot_s.at[turn], cot_r.at[at], (c, to))
 
     def rs_copy(to, at):
         return remote(rs_snd.at[to], rs_rcv.at[at], rs_s.at[to], rs_r.at[at], (c, to))
@@ -161,11 +161,13 @@
         for d in range(1, H):
             build(up(d), h).wait_send()
 
+    partner = t + 1 - 2 * lax.rem(t, 2)
+    for f in range(2, T, 2):
+        cot_copy(lane(f), t, f).start()
+    cot_copy(partner, t, 0).start()
     for d in range(1, H):
         kv_copy(up(d), h).start()
         q_copy(up(d), h).start()
-    for f in range(1, T):
-        cot_copy(lane(f), t).start()
     kv_all[g, h] = kv_snd[h]
     q_rcv[h] = q_snd[h]
 
@@ -179,10 +181,15 @@
     for d in range(H - 1, 0, -1):
         kv_copy(up(d), up(d)).wait_recv()
         forward(up(d))
+        if d == H - 1:
+            for f in range(2, T, 2):
+                cot_copy(lane(f), lane(f), f).wait_recv()
+                cot_copy(partner, lane(f), f + 1).start()
 
     loads[4].wait()
-    for f in range(1, T):
-        cot_copy(lane(f), lane(f)).wait_recv()
+    for f in range(0, T, 2):
+        at = lax.rem(partner + f, T)
+        cot_copy(partner, at, f).wait_recv()
     width = cot.shape[2]
     grad = dot_nt(w_v[:, 0:width], cot[0])
     for i in range(1, T):
@@ -272,13 +279,14 @@
 
     query_total = loop(1, G, back_side, jnp.zeros((HS, Q), F32))
 
-    wait_column(o_copy)
-    mine = turned(jnp.concatenate([o_rcv[i] for i in range(H)], axis=0))
-    for i in range(T):
-        rs_snd[i] = dot_nn(mine, w_v[:, i * width:(i + 1) * width]).astype(BF16)
-    for f in range(1, T):
-        rs_copy(lane(f), t).start()
-    rs_rcv[t] = rs_snd[t]
+    def project():
+        wait_column(o_copy)
+        mine = turned(jnp.concatenate([o_rcv[i] for i in range(H)], axis=0))
+        for i in range(T):
+            rs_snd[i] = dot_nn(mine, w_v[:, i * width:(i + 1) * width]).astype(BF16)
+        for f in range(1, T):
+            rs_copy(lane(f), t).start()
+        rs_rcv[t] = rs_snd[t]
 
     def finish(b, part):
         def gather(e, sofar):
@@ -295,6 +303,8 @@
             finish(b, part[i * F:(i + 1) * F, :])
             if number * len(pair) + i < H - 1:
                 fin_copy(b, h).start()
+        if number == 0:
+            project()
     fin_rcv[h] = fin_snd[h]
     query_out = (query_total * scale).astype(BF16)
     for i in range(H):
@@ -326,8 +336,11 @@
 
     loop(1, G, sent_side, 0)
     for f in range(1, T):
-        cot_copy(lane(f), t).wait_send()
         rs_copy(lane(f), t).wait_send()
+    cot_copy(partner, t, 0).wait_send()
+    for f in range(2, T, 2):
+        cot_copy(lane(f), t, f).wait_send()
+        cot_copy(partner, lane(f), f + 1).wait_send()
 
 
 def store(a, b, c, d, a_out, b_out, c_out, d_out, sem):

time: 27.6 us -> 27 us (0.978)
  Pallas kernels: 26.8 us -> 26.2 us
    pallas_call x1, Pallas kernels: 26 us -> 25.5 us  [step(): pl.pallas_call(functools.partial(kernel, (H, G, T, F)), out_shape=(jax.Sh...]
where the time goes in v4:
time: 27 us; the launch traced here: 26.9 us
  Pallas kernels  26.2 us (97%)
  between operations  0.64 us (2%)
    pallas_call x1, Pallas kernels, step(): pl.pallas_call(functools.partial(kernel, (H, G, T, F)), out_shape=(jax.Sh...  25.5 us
    pallas_call x1, Pallas kernels, step(): pl.pallas_call(store, out_shape=tuple((jax.ShapeDtypeStruct(x.shape, x.dt...  0.74 us

profile of v4, /device:TPU:0, one launch (start us, length us, event | category | flops | bytes accessed | tf_op | source)
XLA Modules:
  0.0 26.9 jit_solution(8268772294954129446)
XLA Ops:
  0.6 25.5 %shard_map.93 = (bf16[128,384]{1,0:T(8,128)(2,1)S(1)}, bf16[128,256]{1,0:T(8,128)(2,1)S(1)}, bf16[128,256]{1,0:T(8,128)(2,1)S(1)}, bf16[128,256]{1,0:T(8,128)(2,1)S(1)}) custom-call(bf16[128,256]{1,0:T(8,128)(2,1)} %q_in.1, bf16[128,256]{1,0:T(8,128)(2,1)} %k_in.1, bf16[128,256]{1,0:T(8,128)(2,1)} %v_in.1, s32[1,128]{1,0:T(1,128)} %bitcast.1, ...), custom_call_target="tpu_custom_call" | custom-call | tf_op jit(solution)/shard_map/pallas_call | solution.py:387
  26.1 0.7 %shard_map.94 = (bf16[128,384]{1,0:T(8,128)(2,1)}, bf16[128,256]{1,0:T(8,128)(2,1)}, bf16[128,256]{1,0:T(8,128)(2,1)}, bf16[128,256]{1,0:T(8,128)(2,1)}) custom-call(bf16[128,384]{1,0:T(8,128)(2,1)S(1)} %get-tuple-element.8.a, bf16[128,256]{1,0:T(8,128)(2,1)S(1)} %get-tuple-element.9.b, bf16[128,256]{1,0:T(8,128)(2,1)S(1)} %get-tuple-element.10.c, ...), custom_call_target="tpu_custom_call" | custom-call | tf_op jit(solution)/shard_map/pallas_call | solution.py:402
